TPU v7x, 32 devices: a whole 2x2x4 slice. The times are simulated.
32 devices in a mesh: dp: 4 (over y, x), fsdp: 8 (over z, core).
Axes of the slice: x: 2, y: 2, z: 4, core: 2. Of those that a mesh axis runs over, the one named last changes fastest.
Arguments:
- hidden: bfloat16 [2, 4608, 4096], P(None, ('dp', 'fsdp')), may hold values from -120 to 120
- cotangent: bfloat16 [2, 4608, 1024], P(None, ('dp', 'fsdp')), may hold values from -6 to 6
- proj_weight: bfloat16 [2, 4096, 1024], P(None, 'fsdp'), may hold values from -3 to 3
- norm_gain: float32 [2, 4096], replicated, may hold values from 0.1 to 1.9
- prev_factor: bfloat16 [2, 512, 128], replicated, may hold values from -0.25 to 0.25
- factor_ranks: int32 [2, 2], replicated, may hold values from 4 to 64, as said below
- layer_order: int32 [2], replicated, may hold values from 0 to 1, each once
Outputs:
- hidden_grad: bfloat16 [4608, 4096], P(('dp', 'fsdp'))
- basis_factor: float32 [2, 4096, 128], P(None, 'fsdp')
Inputs may be any that keep to these rules, and one draw needn't show every extreme that they name: `factor_ranks`: every draw holds a rank equal to 64 and a rank equal to 4.
All inputs are finite; a program needn't handle non-finite values.
Results may differ from a plain program's by a relative error of at most 0.0056.
Values may be sent and summed in bfloat16 or wider, within the bound.
A program may use at most 64 MiB of HBM per device.

v0:
```python
import math
import jax
import jax.numpy as jnp
from jax import lax
from jax.sharding import PartitionSpec as P

D = 4096


def normalize(hidden_rows, gain_row):
    wide_rows = hidden_rows.astype(jnp.float32)
    inverse = lax.rsqrt(jnp.mean(wide_rows * wide_rows, axis=1, keepdims=True) + 1e-05)
    normed = (wide_rows * inverse * gain_row[None, :]).astype(jnp.bfloat16)
    return (inverse, normed)


def masked_factors(factors, rank_pair):
    rank_cols = factors.shape[1] // 2
    position = jnp.arange(2 * rank_cols)
    column = position % rank_cols
    column_limit = jnp.where(position < rank_cols, rank_pair[0], rank_pair[1])
    return jnp.where((column < column_limit)[None, :], factors, jnp.zeros_like(factors))


def project(grad_rows, kept_factor):
    head_cols = grad_rows.shape[1] // 2
    rank_cols = kept_factor.shape[1] // 2
    keys_part = jnp.dot(
        grad_rows[:, :head_cols], kept_factor[:, :rank_cols], preferred_element_type=jnp.float32
    )
    values_part = jnp.dot(
        grad_rows[:, head_cols:], kept_factor[:, rank_cols:], preferred_element_type=jnp.float32
    )
    return jnp.concatenate([keys_part, values_part], axis=1).astype(jnp.bfloat16)


def gram_pair(factor_shard):
    row_count = factor_shard.shape[0]
    rank_cols = factor_shard.shape[1] // 2
    paired = factor_shard.reshape(row_count, 2, rank_cols)
    return jnp.einsum(
        "rmi,rmj->mij",
        paired,
        paired,
        precision=lax.Precision.HIGHEST,
        preferred_element_type=jnp.float32,
    )


def orthonormal(factor_shard, gram_totals, rank_pair):
    rank_cols = factor_shard.shape[1] // 2
    column = jnp.arange(rank_cols)
    pieces = []
    for member in range(2):
        block_cols = factor_shard[:, member * rank_cols : (member + 1) * rank_cols]
        padded = gram_totals[member] + jnp.diag((column >= rank_pair[member]).astype(jnp.float32))
        lower_factor = jnp.linalg.cholesky(padded)
        pieces.append(
            lax.linalg.triangular_solve(
                lower_factor, block_cols, left_side=False, lower=True, transpose_a=True
            )
        )
    return math.sqrt(D) * jnp.concatenate(pieces, axis=1)


def body(hidden, cotangent, proj_weight, norm_gain, prev_factor, factor_ranks, layer_order):
    layer_count = hidden.shape[0]
    top_slot = layer_order[0]
    inverses = []
    shards = []
    basis_list = []
    for slot_index in range(layer_count):
        inverse, normed = normalize(hidden[slot_index], norm_gain[slot_index])
        inverses.append(inverse)
        kept_factor = masked_factors(prev_factor[slot_index], factor_ranks[slot_index])
        projected = project(cotangent[slot_index], kept_factor)
        local_rows = lax.psum_scatter(
            lax.dot_general(
                normed, projected, (((0,), (0,)), ((), ())), preferred_element_type=jnp.float32
            ),
            "fsdp",
            scatter_dimension=0,
            tiled=True,
        )
        factor_shard = lax.psum(local_rows, "dp")
        shards.append(factor_shard)
    stacked = jnp.stack([gram_pair(factor_shard) for factor_shard in shards])
    all_grams = lax.psum(stacked, "fsdp")
    basis_list = [
        orthonormal(shards[slot_index], all_grams[slot_index], factor_ranks[slot_index])
        for slot_index in range(layer_count)
    ]
    top_grads = lax.dynamic_index_in_dim(cotangent, top_slot, 0, keepdims=False)
    top_weight = lax.dynamic_index_in_dim(proj_weight, top_slot, 0, keepdims=False)
    input_grad = lax.dot_general(
        top_grads,
        lax.all_gather(top_weight, "fsdp", axis=0, tiled=True),
        (((1,), (1,)), ((), ())),
        preferred_element_type=jnp.float32,
    )
    top_inverse = lax.dynamic_index_in_dim(jnp.stack(inverses), top_slot, 0, keepdims=False)
    top_gain = lax.dynamic_index_in_dim(norm_gain, top_slot, 0, keepdims=False)
    top_hidden = lax.dynamic_index_in_dim(hidden, top_slot, 0, keepdims=False).astype(jnp.float32)
    scaled = input_grad * top_gain[None, :]
    unit_rows = top_hidden * top_inverse
    inner_mean = jnp.mean(scaled * unit_rows, axis=1, keepdims=True)
    hidden_grad = (top_inverse * (scaled - unit_rows * inner_mean)).astype(jnp.bfloat16)
    return (hidden_grad, jnp.stack(basis_list))


def solution(mesh):
    in_specs = (
        P(None, ("dp", "fsdp"), None),
        P(None, ("dp", "fsdp"), None),
        P(None, "fsdp", None),
        P(),
        P(),
        P(),
        P(),
    )
    out_specs = (P(("dp", "fsdp"), None), P(None, "fsdp", None))
    return jax.shard_map(body, mesh=mesh, in_specs=in_specs, out_specs=out_specs, check_vma=False)
```

profile of v0, /device:TPU:0, one launch (start us, length us, event | category | flops | bytes accessed | tf_op | source)
XLA Modules:
  0.0 299.6 jit_solution(16446004569142756650)
XLA Ops:
  7.2 1.2 slice_bitcast_fusion.1
  8.5 1.4 fusion.76
  9.9 2.4 fusion.71
  12.3 1.0 bitcast_select_fusion.1
  13.9 2.2 fusion.8
  16.2 3.5 %fusion.17 = f32[4096,128]{1,0:T(8,128)} fusion(f32[4096]{0:T(1024)S(1)} %bitcast.139, f32[144]{0:T(256)S(1)} %add_rsqrt_fusion, bf16[2,144,4096]{2,1,0:T(8,128)(2,1)} %param.10, bf16[144,64]{0,1:T(8,128)(2,1)S(1)} %fusion.30, bf16[144,64]{0,1:T(8,128)(2,1)S(1)} %fusion.29), kind=kOutput, calls=%fused_computation.20 | convolution fusion | flops 153427968 | bytes 3330624 | tf_op jit(solution)/shard_map/dot_general | solution.py:78
  20.3 3.5 %fusion.19 = f32[4096,128]{1,0:T(8,128)} fusion(f32[4096]{0:T(1024)S(1)} %bitcast.138, f32[144]{0:T(256)S(1)} %add_rsqrt_fusion.1, bf16[2,144,4096]{2,1,0:T(8,128)(2,1)} %param.10, bf16[144,64]{0,1:T(8,128)(2,1)S(1)} %fusion.28, bf16[144,64]{0,1:T(8,128)(2,1)S(1)} %fusion.27), kind=kOutput, calls=%fused_computation.21 | convolution fusion | flops 153427968 | bytes 3330624 | tf_op jit(solution)/shard_map/dot_general | solution.py:78
  23.8 34.8 %reduce-scatter.5.cloned.1.call-done = f32[512,128]{1,0:T(8,128)} async-done(((f32[4096,128]{1,0:T(8,128)}), f32[512,128]{1,0:T(8,128)}) %reduce-scatter.5.cloned.1.call-update) | async-done | bytes 262160 | tf_op jit(solution)/shard_map/reduce_scatter | solution.py:77
  58.6 37.0 %reduce-scatter.3.cloned.1.call-done = f32[512,128]{1,0:T(8,128)} async-done(((f32[4096,128]{1,0:T(8,128)}), f32[512,128]{1,0:T(8,128)}) %reduce-scatter.3.cloned.1.call-update) | async-done | bytes 262160 | tf_op jit(solution)/shard_map/reduce_scatter | solution.py:77
  95.6 47.0 %all-reduce.6.cloned.1.call-done = (f32[512,128]{1,0:T(8,128)}, f32[512,128]{1,0:T(8,128)}) async-done(((f32[512,128]{1,0:T(8,128)}, f32[512,128]{1,0:T(8,128)}), (f32[512,128]{1,0:T(8,128)}, f32[512,128]{1,0:T(8,128)})) %all-reduce.6.cloned.1.call-update) | async-done | bytes 524304 | tf_op jit(solution)/shard_map/psum | solution.py:85
  142.7 1.1 copy.22
  144.1 1.1 copy.20
  145.6 0.7 pad_maximum_fusion.1
  146.6 1.0 constant_dynamic-slice_fusion.1
  147.6 1.3 compare_convert_fusion.2
  148.9 1.2 compare_convert_fusion
  150.1 51.2 %all-reduce.4.cloned.1.call-done = f32[2,2,64,64]{2,3,1,0:T(8,128)} async-done(((f32[2,2,64,64]{2,3,1,0:T(8,128)}), f32[2,2,64,64]{2,3,1,0:T(8,128)}) %all-reduce.4.cloned.1.call-update) | async-done | bytes 65552 | tf_op jit(solution)/shard_map/psum | solution.py:88
  201.4 0.8 fusion.60
  202.3 5.8 %cholesky.107 = f32[64,64]{1,0:T(8,128)S(1)} custom-call(f32[64,64]{1,0:T(8,128)S(1)} %fusion.62), custom_call_target="Cholesky" | custom-call | tf_op jit(solution)/shard_map/jit(cholesky)/cholesky | solution.py:57
  208.8 0.7 fusion.56
  209.5 4.9 %custom-call.11 = f32[1,64,64]{1,2,0:T(8,128)S(1)} custom-call(f32[1,64,64]{2,1,0:T(8,128)S(1)} %fusion.56), custom_call_target="InvertDiagBlocksLowerTriangular" | custom-call | tf_op jit(solution)/shard_map/triangular_solve/custom-call.0 | solution.py:59
  214.5 5.8 %cholesky.96 = f32[64,64]{1,0:T(8,128)S(1)} custom-call(f32[64,64]{1,0:T(8,128)S(1)} %fusion.64), custom_call_target="Cholesky" | custom-call | tf_op jit(solution)/shard_map/jit(cholesky)/cholesky | solution.py:57
  221.7 4.9 %custom-call.10 = f32[1,64,64]{1,2,0:T(8,128)S(1)} custom-call(f32[1,64,64]{2,1,0:T(8,128)S(1)} %fusion.55), custom_call_target="InvertDiagBlocksLowerTriangular" | custom-call | tf_op jit(solution)/shard_map/triangular_solve/custom-call.0 | solution.py:59
  226.7 5.8 %cholesky.85 = f32[64,64]{1,0:T(8,128)S(1)} custom-call(f32[64,64]{1,0:T(8,128)S(1)} %fusion.66), custom_call_target="Cholesky" | custom-call | tf_op jit(solution)/shard_map/jit(cholesky)/cholesky | solution.py:57
  233.9 4.9 %custom-call.9 = f32[1,64,64]{1,2,0:T(8,128)S(1)} custom-call(f32[1,64,64]{2,1,0:T(8,128)S(1)} %fusion.54), custom_call_target="InvertDiagBlocksLowerTriangular" | custom-call | tf_op jit(solution)/shard_map/triangular_solve/custom-call.0 | solution.py:59
  238.9 5.8 %cholesky.74 = f32[64,64]{1,0:T(8,128)S(1)} custom-call(f32[64,64]{1,0:T(8,128)S(1)} %fusion.68), custom_call_target="Cholesky" | custom-call | tf_op jit(solution)/shard_map/jit(cholesky)/cholesky | solution.py:57
  245.4 0.7 fusion.53
  246.1 4.9 %custom-call.8 = f32[1,64,64]{1,2,0:T(8,128)S(1)} custom-call(f32[1,64,64]{2,1,0:T(8,128)S(1)} %fusion.53), custom_call_target="InvertDiagBlocksLowerTriangular" | custom-call | tf_op jit(solution)/shard_map/triangular_solve/custom-call.0 | solution.py:59
  253.0 1.0 copy.28
  254.0 30.6 %all-gather.3.cloned.1.call-done = bf16[1,4096,1024]{2,1,0:T(8,128)(2,1)} async-done(((bf16[1,512,1024]{2,1,0:T(8,128)(2,1)}), bf16[1,4096,1024]{2,1,0:T(8,128)(2,1)}) %all-gather.3.cloned.1.call-update) | async-done | bytes 8388624 | tf_op jit(solution)/shard_map/all_gather | solution.py:97
  284.6 6.9 %fusion.13 = (f32[144]{0:T(256)S(1)}, f32[144,4096]{1,0:T(8,128)S(1)}) fusion(f32[144]{0:T(256)S(1)} %bitcast.141, bf16[2,144,4096]{2,1,0:T(8,128)(2,1)} %param.10, s32[]{:T(128)S(6)} %select_n.69, f32[4096]{0:T(1024)S(1)} %bitcast.140, bf16[1,4096,1024]{2,1,0:T(8,128)(2,1)} %all-gather.3.cloned.1.call-done, bf16[2,144,1024]{2,1,0:T(8,128)(2,1)S(1)} %copy-done.4), kind=kOutput, calls=%fused_computation.16 | convolution fusion | flops 1210908544 | bytes 12241472 | tf_op jit(solution)/shard_map/dot_general | solution.py:95
  291.5 1.6 fusion.16
  (60 shorter events, 8.8 us)
Async XLA Ops:
  7.2 139.4 %copy-start = (bf16[2,512,1024]{2,1,0:T(8,128)(2,1)S(1)}, bf16[2,512,1024]{2,1,0:T(8,128)(2,1)}, u32[]{:S(2)}) copy-start(bf16[2,512,1024]{2,1,0:T(8,128)(2,1)} %param.12) | copy-start | bytes 6291460
  7.2 6.7 %copy-start.6 = (s32[2]{0:T(128)S(1)}, s32[2]{0:T(128)}, u32[]{:S(2)}) copy-start(s32[2]{0:T(128)} %param.16) | copy-start | bytes 28
  7.2 9.0 %copy-start.5 = (f32[2,4096]{1,0:T(2,128)S(1)}, f32[2,4096]{1,0:T(2,128)}, u32[]{:S(2)}) copy-start(f32[2,4096]{1,0:T(2,128)} %param.13) | copy-start | bytes 98308
  7.2 51.4 %reduce-scatter.5.cloned.1.call-start = ((), (), s32[]{:S(2)}) async-start(), calls=%async_computation.3 | async-start | bytes 2359296 | tf_op jit(solution)/shard_map/reduce_scatter | solution.py:77
  19.7 75.8 %reduce-scatter.3.cloned.1.call-start = ((), (), s32[]{:S(2)}) async-start(), calls=%async_computation.2 | async-start | bytes 2359296 | tf_op jit(solution)/shard_map/reduce_scatter | solution.py:77
  23.8 118.9 %all-reduce.6.cloned.1.call-start = ((), (), s32[]{:S(2)}) async-start(), calls=%async_computation.6 | async-start | bytes 1048576 | tf_op jit(solution)/shard_map/psum | solution.py:85
  95.6 105.8 %all-reduce.4.cloned.1.call-start = ((), (), s32[]{:S(2)}) async-start(), calls=%async_computation.4 | async-start | bytes 262144 | tf_op jit(solution)/shard_map/psum | solution.py:88
  146.3 104.7 %copy-start.3 = (f32[512,128]{1,0:T(8,128)S(1)}, f32[512,128]{1,0:T(8,128)}, u32[]{:S(2)}) copy-start(f32[512,128]{1,0:T(8,128)} %get-tuple-element.10) | copy-start | bytes 786436
  146.3 138.2 %all-gather.3.cloned.1.call-start = ((), (), s32[]{:S(2)}) async-start(), calls=%async_computation.5 | async-start | bytes 9437184 | tf_op jit(solution)/shard_map/all_gather | solution.py:97
  147.6 104.4 %copy-start.2 = (f32[512,128]{1,0:T(8,128)S(1)}, f32[512,128]{1,0:T(8,128)}, u32[]{:S(2)}) copy-start(f32[512,128]{1,0:T(8,128)} %get-tuple-element.11) | copy-start | bytes 786436
  251.0 33.6 %copy-start.4 = (bf16[2,144,1024]{2,1,0:T(8,128)(2,1)S(1)}, bf16[2,144,1024]{2,1,0:T(8,128)(2,1)}, u32[]{:S(2)}) copy-start(bf16[2,144,1024]{2,1,0:T(8,128)(2,1)} %param.11) | copy-start | bytes 1769476
  284.6 6.9 %copy-start.1 = (bf16[2,144,4096]{2,1,0:T(8,128)(2,1)S(1)}, bf16[2,144,4096]{2,1,0:T(8,128)(2,1)}, u32[]{:S(2)}) copy-start(bf16[2,144,4096]{2,1,0:T(8,128)(2,1)} %param.10) | copy-start | bytes 7077892
Sparse Core Ops, SparseCore 0:
  19.9 38.7 reduce-scatter.4
  60.9 34.6 reduce-scatter.2
  98.6 44.0 all-reduce.5
  146.4 54.8 all-reduce.3
  203.4 81.1 all-gather.2
where the time goes:
time: 300 us
  waiting for transfers between devices  201 us (67%)
  other arithmetic  59.6 us (20%)
  matrix products  17.6 us (6%)
  between operations  14.2 us (5%)
  local copies, waits for them, and re-layouts  7.26 us (2%)
    reduce_scatter x2, waiting for transfers between devices, body(): lax.psum_scatter(lax.dot_general(normed, projected, (((0,), (0,)), ((), (...  71.7 us
    psum x1, waiting for transfers between devices, body(): all_grams = lax.psum(stacked, 'fsdp')  51.2 us
    psum x1, waiting for transfers between devices, body(): factor_shard = lax.psum(local_rows, 'dp')  47 us
    all_gather x1, waiting for transfers between devices, body(): lax.all_gather(top_weight, 'fsdp', axis=0, tiled=True)  30.6 us
    another operation x12, other arithmetic, orthonormal(): lower_factor = jnp.linalg.cholesky(padded)  26.1 us
    another operation x8, other arithmetic, orthonormal(): lax.linalg.triangular_solve(lower_factor, block_cols, left_side=False, lo...  22.2 us
    dot_general x2, matrix products, body(): lax.dot_general(normed, projected, (((0,), (0,)), ((), ())), preferred_el...  6.96 us
    dot_general x1, matrix products, body(): lax.dot_general(top_grads, lax.all_gather(top_weight, 'fsdp', axis=0, til...  6.9 us
  transfers between devices with their start and end apart: 5, of which 5 were waited for; matrix products, arithmetic and copies ran while one was open for 20% of the time, Pallas kernels for 0%

commit v1 on v0

--- a/solution.py
+++ b/solution.py
@@ -85,7 +85,8 @@
         factor_shard = lax.psum(local_rows, "dp")
         shards.append(factor_shard)
     stacked = jnp.stack([gram_pair(factor_shard) for factor_shard in shards])
-    all_grams = lax.psum(stacked, "fsdp")
+    expand_sections_now = lambda u_in: lax.all_gather(u_in, "fsdp").sum(axis=0)
+    all_grams = expand_sections_now(stacked)
     basis_list = [
         orthonormal(shards[slot_index], all_grams[slot_index], factor_ranks[slot_index])
         for slot_index in range(layer_count)

time: 300 us -> 245 us (0.82)
  waiting for transfers between devices: 201 us -> 117 us
  blocking collectives: 0 us -> 20.5 us
  other arithmetic: 59.6 us -> 66.8 us
    psum x1 -> x0, waiting for transfers between devices: 51.2 us -> none  [body(): all_grams = lax.psum(stacked, 'fsdp')]
    all_gather x1, waiting for transfers between devices: 30.6 us -> 4.72 us  [body(): lax.all_gather(top_weight, 'fsdp', axis=0, tiled=True)]
    all_gather x0 -> x1, blocking collectives: none -> 20.5 us  [body(): expand_sections_now = lambda u_in: lax.all_gather(u_in, 'fsdp').sum(axis=0)]
    psum x1, waiting for transfers between devices: 47 us -> 40.4 us  [body(): factor_shard = lax.psum(local_rows, 'dp')]
  transfers between devices with their start and end apart: 5 -> 4, of which waited for: 5 -> 4; matrix products, arithmetic and copies ran while one was open for 20% -> 29% of each run, Pallas kernels for 0% -> 0%
where the time goes in v1:
time: 245 us
  waiting for transfers between devices  117 us (48%)
  other arithmetic  66.8 us (27%)
  blocking collectives  20.5 us (8%)
  matrix products  18.5 us (8%)
  between operations  14.2 us (6%)
  local copies, waits for them, and re-layouts  7.64 us (3%)
    reduce_scatter x2, waiting for transfers between devices, body(): lax.psum_scatter(lax.dot_general(normed, projected, (((0,), (0,)), ((), (...  71.8 us
    psum x1, waiting for transfers between devices, body(): factor_shard = lax.psum(local_rows, 'dp')  40.4 us
    another operation x12, other arithmetic, orthonormal(): lower_factor = jnp.linalg.cholesky(padded)  26.1 us
    another operation x8, other arithmetic, orthonormal(): lax.linalg.triangular_solve(lower_factor, block_cols, left_side=False, lo...  22.2 us
    all_gather x1, blocking collectives, body(): expand_sections_now = lambda u_in: lax.all_gather(u_in, 'fsdp').sum(axis=0)  20.5 us
    dot_general x2, matrix products, body(): lax.dot_general(normed, projected, (((0,), (0,)), ((), ())), preferred_el...  6.96 us
    dot_general x1, matrix products, body(): lax.dot_general(top_grads, lax.all_gather(top_weight, 'fsdp', axis=0, til...  6.9 us
  transfers between devices with their start and end apart: 4, of which 4 were waited for; matrix products, arithmetic and copies ran while one was open for 29% of the time, Pallas kernels for 0%

profile of v1, /device:TPU:0, one launch (start us, length us, event | category | flops | bytes accessed | tf_op | source)
XLA Modules:
  0.0 244.8 jit_solution(5310999981650866182)
XLA Ops:
  7.2 1.2 slice_bitcast_fusion.1
  8.5 1.5 fusion.73
  10.0 2.6 %fusion.67 = (pred[128]{0:T(512)(128)(4,1)S(1)}, pred[128]{0:T(512)(128)(4,1)S(1)}) fusion(s32[]{:T(128)} %bitcast.13, s32[]{:T(128)} %bitcast.12, s32[]{:T(128)} %bitcast.23, s32[]{:T(128)} %bitcast.22), kind=kLoop, calls=%fused_computation.122 | loop fusion | flops 1408 | bytes 272 | tf_op jit(solution)/shard_map/lt | solution.py:22
  12.6 1.0 bitcast_select_fusion.1
  14.1 2.2 fusion.8
  16.4 3.5 %fusion.17 = f32[4096,128]{1,0:T(8,128)} fusion(f32[4096]{0:T(1024)S(1)} %bitcast.141, f32[144]{0:T(256)S(1)} %add_rsqrt_fusion, bf16[2,144,4096]{2,1,0:T(8,128)(2,1)} %param.10, bf16[144,64]{0,1:T(8,128)(2,1)S(1)} %fusion.30, bf16[144,64]{0,1:T(8,128)(2,1)S(1)} %fusion.29), kind=kOutput, calls=%fused_computation.20 | convolution fusion | flops 153427968 | bytes 3330624 | tf_op jit(solution)/shard_map/dot_general | solution.py:78
  20.5 3.5 %fusion.19 = f32[4096,128]{1,0:T(8,128)} fusion(f32[4096]{0:T(1024)S(1)} %bitcast.140, f32[144]{0:T(256)S(1)} %add_rsqrt_fusion.1, bf16[2,144,4096]{2,1,0:T(8,128)(2,1)} %param.10, bf16[144,64]{0,1:T(8,128)(2,1)S(1)} %fusion.28, bf16[144,64]{0,1:T(8,128)(2,1)S(1)} %fusion.27), kind=kOutput, calls=%fused_computation.21 | convolution fusion | flops 153427968 | bytes 3330624 | tf_op jit(solution)/shard_map/dot_general | solution.py:78
  24.1 34.8 %reduce-scatter.5.cloned.1.call-done = f32[512,128]{1,0:T(8,128)} async-done(((f32[4096,128]{1,0:T(8,128)}), f32[512,128]{1,0:T(8,128)}) %reduce-scatter.5.cloned.1.call-update) | async-done | bytes 262160 | tf_op jit(solution)/shard_map/reduce_scatter | solution.py:77
  58.8 37.0 %reduce-scatter.3.cloned.1.call-done = f32[512,128]{1,0:T(8,128)} async-done(((f32[4096,128]{1,0:T(8,128)}), f32[512,128]{1,0:T(8,128)}) %reduce-scatter.3.cloned.1.call-update) | async-done | bytes 262160 | tf_op jit(solution)/shard_map/reduce_scatter | solution.py:77
  95.9 1.0 constant_dynamic-slice_fusion.1
  97.0 1.2 compare_convert_fusion
  98.2 1.3 compare_convert_fusion.1
  99.4 1.2 compare_convert_fusion.2
  100.7 1.2 compare_convert_fusion.3
  102.5 40.4 %all-reduce.3.cloned.1.call-done = (f32[512,128]{1,0:T(8,128)}, f32[512,128]{1,0:T(8,128)}) async-done(((f32[512,128]{1,0:T(8,128)}, f32[512,128]{1,0:T(8,128)}), (f32[512,128]{1,0:T(8,128)}, f32[512,128]{1,0:T(8,128)})) %all-reduce.3.cloned.1.call-update) | async-done | bytes 524304 | tf_op jit(solution)/shard_map/psum | solution.py:85
  142.9 1.1 copy.26
  144.0 1.1 copy.25
  145.8 20.5 %all-gather.1 = f32[16,2,64,64]{3,2,1,0:T(8,128)S(1)} all-gather(f32[2,2,64,64]{3,2,1,0:T(8,128)S(1)} %pad_maximum_fusion.1), channel_id=3, replica_groups=mesh['dp'=4,'fsdp'=8] {'fsdp'}, dimensions={0}, use_global_device_ids=true | all-gather | bytes 589824 | tf_op jit(solution)/shard_map/all_gather | solution.py:88
  166.5 0.7 bitcast_add_fusion.1
  168.0 5.8 %cholesky.107 = f32[64,64]{1,0:T(8,128)S(1)} custom-call(f32[64,64]{1,0:T(8,128)S(1)} %fusion.58), custom_call_target="Cholesky" | custom-call | tf_op jit(solution)/shard_map/jit(cholesky)/cholesky | solution.py:57
  175.2 4.9 %custom-call.11 = f32[1,64,64]{1,2,0:T(8,128)S(1)} custom-call(f32[1,64,64]{2,1,0:T(8,128)S(1)} %fusion.56), custom_call_target="InvertDiagBlocksLowerTriangular" | custom-call | tf_op jit(solution)/shard_map/triangular_solve/custom-call.0 | solution.py:59
  181.6 5.8 %cholesky.96 = f32[64,64]{1,0:T(8,128)S(1)} custom-call(f32[64,64]{1,0:T(8,128)S(1)} %fusion.60), custom_call_target="Cholesky" | custom-call | tf_op jit(solution)/shard_map/jit(cholesky)/cholesky | solution.py:57
  188.8 4.9 %custom-call.10 = f32[1,64,64]{1,2,0:T(8,128)S(1)} custom-call(f32[1,64,64]{2,1,0:T(8,128)S(1)} %fusion.55), custom_call_target="InvertDiagBlocksLowerTriangular" | custom-call | tf_op jit(solution)/shard_map/triangular_solve/custom-call.0 | solution.py:59
  195.2 5.8 %cholesky.85 = f32[64,64]{1,0:T(8,128)S(1)} custom-call(f32[64,64]{1,0:T(8,128)S(1)} %fusion.62), custom_call_target="Cholesky" | custom-call | tf_op jit(solution)/shard_map/jit(cholesky)/cholesky | solution.py:57
  202.4 4.9 %custom-call.9 = f32[1,64,64]{1,2,0:T(8,128)S(1)} custom-call(f32[1,64,64]{2,1,0:T(8,128)S(1)} %fusion.54), custom_call_target="InvertDiagBlocksLowerTriangular" | custom-call | tf_op jit(solution)/shard_map/triangular_solve/custom-call.0 | solution.py:59
  208.9 5.8 %cholesky.74 = f32[64,64]{1,0:T(8,128)S(1)} custom-call(f32[64,64]{1,0:T(8,128)S(1)} %fusion.64), custom_call_target="Cholesky" | custom-call | tf_op jit(solution)/shard_map/jit(cholesky)/cholesky | solution.py:57
  216.0 4.9 %custom-call.8 = f32[1,64,64]{1,2,0:T(8,128)S(1)} custom-call(f32[1,64,64]{2,1,0:T(8,128)S(1)} %fusion.53), custom_call_target="InvertDiagBlocksLowerTriangular" | custom-call | tf_op jit(solution)/shard_map/triangular_solve/custom-call.0 | solution.py:59
  221.0 1.5 convolution_bitcast_fusion
  224.0 1.0 copy.35
  225.0 4.7 %all-gather.4.cloned.1.call-done = bf16[1,4096,1024]{2,1,0:T(8,128)(2,1)} async-done(((bf16[1,512,1024]{2,1,0:T(8,128)(2,1)}), bf16[1,4096,1024]{2,1,0:T(8,128)(2,1)}) %all-gather.4.cloned.1.call-update) | async-done | bytes 8388624 | tf_op jit(solution)/shard_map/all_gather | solution.py:98
  229.7 6.9 %fusion.13 = (f32[144]{0:T(256)S(1)}, f32[144,4096]{1,0:T(8,128)S(1)}) fusion(f32[144]{0:T(256)S(1)} %bitcast.143, bf16[2,144,4096]{2,1,0:T(8,128)(2,1)} %param.10, s32[]{:T(128)S(6)} %select_n.69, f32[4096]{0:T(1024)S(1)} %bitcast.142, bf16[1,4096,1024]{2,1,0:T(8,128)(2,1)} %all-gather.4.cloned.1.call-done, bf16[2,144,1024]{2,1,0:T(8,128)(2,1)S(1)} %copy-done.4), kind=kOutput, calls=%fused_computation.16 | convolution fusion | flops 1210908544 | bytes 12241472 | tf_op jit(solution)/shard_map/dot_general | solution.py:96
  236.7 1.6 fusion.16
  (71 shorter events, 15.0 us)
Async XLA Ops:
  7.2 88.7 %copy-start = (bf16[2,512,1024]{2,1,0:T(8,128)(2,1)S(1)}, bf16[2,512,1024]{2,1,0:T(8,128)(2,1)}, u32[]{:S(2)}) copy-start(bf16[2,512,1024]{2,1,0:T(8,128)(2,1)} %param.12) | copy-start | bytes 6291460
  7.2 6.9 %copy-start.7 = (s32[2]{0:T(128)S(1)}, s32[2]{0:T(128)}, u32[]{:S(2)}) copy-start(s32[2]{0:T(128)} %param.16) | copy-start | bytes 28
  7.2 9.2 %copy-start.5 = (f32[2,4096]{1,0:T(2,128)S(1)}, f32[2,4096]{1,0:T(2,128)}, u32[]{:S(2)}) copy-start(f32[2,4096]{1,0:T(2,128)} %param.13) | copy-start | bytes 98308
  7.2 51.6 %reduce-scatter.5.cloned.1.call-start = ((), (), s32[]{:S(2)}) async-start(), calls=%async_computation.3 | async-start | bytes 2359296 | tf_op jit(solution)/shard_map/reduce_scatter | solution.py:77
  20.0 75.9 %reduce-scatter.3.cloned.1.call-start = ((), (), s32[]{:S(2)}) async-start(), calls=%async_computation.2 | async-start | bytes 2359296 | tf_op jit(solution)/shard_map/reduce_scatter | solution.py:77
  24.0 118.9 %all-reduce.3.cloned.1.call-start = ((), (), s32[]{:S(2)}) async-start(), calls=%async_computation.5 | async-start | bytes 1048576 | tf_op jit(solution)/shard_map/psum | solution.py:85
  95.8 133.9 %all-gather.4.cloned.1.call-start = ((), (), s32[]{:S(2)}) async-start(), calls=%async_computation.4 | async-start | bytes 9437184 | tf_op jit(solution)/shard_map/all_gather | solution.py:98
  166.3 56.7 %copy-start.2 = (f32[512,128]{1,0:T(8,128)S(1)}, f32[512,128]{1,0:T(8,128)}, u32[]{:S(2)}) copy-start(f32[512,128]{1,0:T(8,128)} %get-tuple-element.13) | copy-start | bytes 786436
  166.4 56.1 %copy-start.3 = (f32[512,128]{1,0:T(8,128)S(1)}, f32[512,128]{1,0:T(8,128)}, u32[]{:S(2)}) copy-start(f32[512,128]{1,0:T(8,128)} %get-tuple-element.12) | copy-start | bytes 786436
  220.9 8.8 %copy-start.4 = (bf16[2,144,1024]{2,1,0:T(8,128)(2,1)S(1)}, bf16[2,144,1024]{2,1,0:T(8,128)(2,1)}, u32[]{:S(2)}) copy-start(bf16[2,144,1024]{2,1,0:T(8,128)(2,1)} %param.11) | copy-start | bytes 1769476
  221.0 8.8 %copy-start.6 = (f32[1,144,1]{1,2,0:T(1,128)S(1)}, f32[1,144,1]{1,2,0:T(1,128)}, u32[]{:S(2)}) copy-start(f32[1,144,1]{1,2,0:T(1,128)} %fusion.66) | copy-start | bytes 1732
  229.7 6.9 %copy-start.1 = (bf16[2,144,4096]{2,1,0:T(8,128)(2,1)S(1)}, bf16[2,144,4096]{2,1,0:T(8,128)(2,1)}, u32[]{:S(2)}) copy-start(bf16[2,144,4096]{2,1,0:T(8,128)(2,1)} %param.10) | copy-start | bytes 7077892
Sparse Core Ops, SparseCore 0:
  20.1 38.7 reduce-scatter.4
  61.1 34.6 reduce-scatter.2
  98.8 44.0 all-reduce.2
  144.9 84.7 all-gather.3
